TPU v7x, 512 devices: a whole 4x4x16 slice. The times are simulated.
512 devices in a mesh: grp: 64 (over y_lo, z, core), tp: 8 (over x, y_hi).
Axes of the slice: x: 4, y: 4 (y_hi: 2, y_lo: 2; y = y_hi * 2 + y_lo), z: 16, core: 2. Of those that a mesh axis runs over, the one named last changes fastest.
Arguments:
- queries: bfloat16 [64, 2, 512, 2048], P('grp', None, None, 'tp'), may hold values from -9 to 9
- fresh_kv: bfloat16 [64, 2, 512, 2, 2048], P('grp', None, None, None, 'tp'), may hold values from -9 to 9
- stale_kv: bfloat16 [64, 2, 512, 2, 2048], P('grp', None, None, None, 'tp'), may hold values from -6 to 6
- text_kv: bfloat16 [64, 2, 256, 2, 2048], P('grp', None, None, None, 'tp'), may hold values from -6 to 6
- w_velocity: bfloat16 [2048, 64], P('tp'), may hold values from -2.390625 to 2.390625
- latent: float32 [64, 2, 512, 64], P('grp', None, 'tp'), may hold values from -6 to 6
- live_counts: int32 [64, 2], replicated, may hold values from 128 to 512, as said below
- refresh_rows: int32 [64, 2, 64], replicated, may hold values from 0 to 511, as said below
- request_list: int32 [64], replicated, may hold values from 0 to 63, each once
- timesteps: int32 [64, 2], replicated, may hold values from 0 to 999, as said below
Outputs:
- next_stale: bfloat16 [64, 2, 512, 2, 2048], P('grp', None, None, None, 'tp')
- velocity: float32 [64, 2, 512, 64], P('grp', None, 'tp')
- latent_next: float32 [64, 2, 512, 64], P('grp', None, 'tp')
Inputs may be any that keep to these rules, and one draw needn't show every extreme that they name: `live_counts`: 512 is reached in every draw. `refresh_rows`: rows within one list are distinct. `timesteps`: the next timestep is below the current one. `request_list`: each request appears once.
All inputs are finite; a program needn't handle non-finite values.
Results may differ from a plain program's by a relative error of at most 0.0045.
Values may be sent and summed in bfloat16 or wider, within the bound.
A program may use at most 64 MiB of HBM per device.

v0:
```python
import math
import jax
import jax.numpy as jnp
from jax import lax
from jax.sharding import PartitionSpec as P

HD = 128


def from_behind(block, axis, distance):
    devices = range(lax.axis_size(axis))
    route = [((i - distance) % len(devices), i) for i in devices]
    return lax.ppermute(block, axis, route)


def slot_velocity(slot_query, own_kv, partner_kv, text_pair, own_live, partner_live, w_velocity):
    img_rows = slot_query.shape[0]
    heads_here = slot_query.shape[1] // HD
    key_rows = jnp.concatenate([own_kv[:, 0], partner_kv[:, 0], text_pair[:, 0]], axis=0)
    value_rows = jnp.concatenate([own_kv[:, 1], partner_kv[:, 1], text_pair[:, 1]], axis=0)
    row_ids = jnp.arange(img_rows, dtype=jnp.int32)
    live_mask = jnp.concatenate(
        [row_ids < own_live, row_ids < partner_live, jnp.ones((text_pair.shape[0],), dtype=bool)]
    )
    outputs = []
    for head_index in range(heads_here):
        first = head_index * HD
        scores = lax.dot_general(
            slot_query[:, first : first + HD],
            key_rows[:, first : first + HD],
            (((1,), (1,)), ((), ())),
            preferred_element_type=jnp.float32,
        ) * (1.0 / math.sqrt(HD))
        scores = jnp.where(live_mask[None, :], scores, -jnp.inf)
        row_top = jnp.max(scores, axis=1, keepdims=True)
        weights = jnp.exp(scores - row_top)
        totals = jnp.sum(weights, axis=1, keepdims=True)
        blended = (
            jnp.dot(
                weights.astype(jnp.bfloat16),
                value_rows[:, first : first + HD],
                preferred_element_type=jnp.float32,
            )
            / totals
        )
        outputs.append(blended.astype(jnp.bfloat16))
    blended = jnp.concatenate(outputs, axis=1)
    return jnp.dot(blended, w_velocity, preferred_element_type=jnp.float32)


def shards(
    queries,
    fresh_kv,
    stale_kv,
    text_kv,
    w_velocity,
    latent,
    live_counts,
    refresh_rows,
    request_list,
    timesteps,
):
    groups_count = lax.axis_size("grp")
    half_groups = groups_count // 2
    my_group = lax.axis_index("grp")
    partner = (my_group + half_groups) % groups_count
    slot_count = queries.shape[1]
    partner_fresh = from_behind(fresh_kv, "grp", half_groups)
    text_other = from_behind(text_kv, "grp", half_groups)
    partner_lists = lax.dynamic_index_in_dim(refresh_rows, partner, 0, keepdims=False)
    my_live = lax.dynamic_index_in_dim(live_counts, my_group, 0, keepdims=False)
    partner_live = lax.dynamic_index_in_dim(live_counts, partner, 0, keepdims=False)
    arrived = jnp.stack(
        [
            jnp.take(partner_fresh[0, slot_index], partner_lists[slot_index], axis=0)
            for slot_index in range(slot_count)
        ]
    )
    partials = []
    for slot_index in range(slot_count):
        repaired = stale_kv[0, slot_index].at[partner_lists[slot_index]].set(arrived[slot_index])
        text_pair = jnp.concatenate([text_kv[0, slot_index], text_other[0, slot_index]], axis=0)
        partials.append(
            slot_velocity(
                queries[0, slot_index],
                fresh_kv[0, slot_index],
                repaired,
                text_pair,
                my_live[slot_index],
                partner_live[slot_index],
                w_velocity,
            )
        )
    partial_value = jnp.stack(partials)
    tp_count = lax.axis_size("tp")
    share = partial_value.shape[1] // tp_count
    tp_index = lax.axis_index("tp")
    whole = lax.psum(partial_value, "tp")
    summed = lax.dynamic_slice_in_dim(whole, tp_index * share, share, 1)
    row_ids = tp_index * share + jnp.arange(share, dtype=jnp.int32)
    live_rows = row_ids[None, :] < my_live[:, None]
    velocity = jnp.where(live_rows[:, :, None], summed, 0.0)
    pair_index = my_group % half_groups
    request_ids = lax.dynamic_slice_in_dim(request_list, pair_index * slot_count, slot_count)
    matches = (
        request_ids[:, None] == jnp.arange(timesteps.shape[0], dtype=jnp.int32)[None, :]
    ).astype(jnp.int32)
    times = jnp.dot(matches, timesteps)
    step_size = (times[:, 1] - times[:, 0]).astype(jnp.float32) / 1000.0
    latent_next = latent[0] + step_size[:, None, None] * velocity
    return (partner_fresh, velocity[None], latent_next[None])


def solution(mesh):
    return jax.shard_map(
        shards,
        mesh=mesh,
        in_specs=(
            P("grp", None, None, "tp"),
            P("grp", None, None, None, "tp"),
            P("grp", None, None, None, "tp"),
            P("grp", None, None, None, "tp"),
            P("tp", None),
            P("grp", None, "tp", None),
            P(),
            P(),
            P(),
            P(),
        ),
        out_specs=(
            P("grp", None, None, None, "tp"),
            P("grp", None, "tp", None),
            P("grp", None, "tp", None),
        ),
        check_vma=False,
    )
```

profile of v0, /device:TPU:32, one launch (start us, length us, event | category | flops | bytes accessed | tf_op | source)
XLA Modules:
  0.0 191.7 jit_solution(1452022395850017873)
XLA Ops:
  7.3 1.2 copy.61
  8.5 3.5 %collective-permute-start.1 = (bf16[1,2,256,2,256]{4,2,3,1,0:T(8,128)(2,1)S(1)}, bf16[1,2,256,2,256]{4,2,3,1,0:T(8,128)(2,1)}, u32[]{:S(2)}, u32[]{:S(2)}) collective-permute-start(bf16[1,2,256,2,256]{4,2,3,1,0:T(8,128)(2,1)S(1)} %copy.61), channel_id=1, source_target_pairs={{256,0},{264,8},{272,16},{280,24},{288,32},{296,40},{304,48},{312,... | collective-permute-start | bytes 1572872 | tf_op jit(solution)/shard_map/ppermute | solution.py:13
  12.0 2.4 %collective-permute-start = (bf16[1,2,512,2,256]{4,3,2,1,0:T(2,128)(2,1)}, bf16[1,2,512,2,256]{4,3,2,1,0:T(2,128)(2,1)S(1)}, u32[]{:S(2)}, u32[]{:S(2)}) collective-permute-start(bf16[1,2,512,2,256]{4,3,2,1,0:T(2,128)(2,1)} %param.13), channel_id=1, source_target_pairs={{256,0},{264,8},{272,16},{280,24},{288,32},{296,40},{304,48},{312,... | collective-permute-start | bytes 3145736 | tf_op jit(solution)/shard_map/ppermute | solution.py:13
  15.4 0.8 slice_bitcast_fusion.10
  16.3 1.9 %fusion.83 = (bf16[1,1,512,2,256]{4,3,2,1,0:T(2,128)(2,1)S(1)}, bf16[1,1,512,2,256]{4,3,2,1,0:T(2,128)(2,1)S(1)}) fusion(bf16[1,2,512,2,256]{4,3,2,1,0:T(2,128)(2,1)} %param.13), kind=kLoop, calls=%fused_computation.132 | loop fusion | bytes 2097152 | tf_op jit(solution)/shard_map/slice | solution.py:86
  18.5 0.8 multiply_reduce_fusion
  19.2 0.7 fusion.82
  22.4 0.8 slice_bitcast_fusion.13
  23.4 0.9 slice_bitcast_fusion.4
  24.2 0.7 iota_compare_fusion.2
  24.9 0.7 slice_bitcast_fusion.8
  25.7 2.7 %slice_bitcast_fusion.3 = (bf16[512,2,256]{2,1,0:T(2,128)(2,1)S(1)}, bf16[512,2,256]{2,1,0:T(2,128)(2,1)}) fusion(bf16[1,2,512,2,256]{4,3,2,1,0:T(2,128)(2,1)} %param.14), kind=kLoop, calls=%fused_computation.55 | loop fusion | bytes 2097152 | tf_op jit(solution)/shard_map/squeeze | solution.py:81
  28.4 1.1 slice_bitcast_fusion.9
  29.5 0.9 fusion.60
  30.4 16.1 %collective-permute-done = bf16[1,2,512,2,256]{4,3,2,1,0:T(2,128)(2,1)S(1)} collective-permute-done((bf16[1,2,512,2,256]{4,3,2,1,0:T(2,128)(2,1)}, bf16[1,2,512,2,256]{4,3,2,1,0:T(2,128)(2,1)S(1)}, u32[]{:S(2)}, u32[]{:S(2)}) %collective-permute-start) | collective-permute-done | bytes 1048608 | tf_op jit(solution)/shard_map/ppermute | solution.py:13
  46.5 1.5 slice_bitcast_fusion.1
  48.0 1.8 gather_fusion
  49.8 0.7 gather_fusion.1
  50.5 0.9 broadcast_select_fusion
  51.4 2.6 %scatter_fusion = bf16[512,2,256]{2,1,0:T(2,128)(2,1)S(1)} fusion(bf16[512,2,256]{2,1,0:T(2,128)(2,1)S(1)} %get-tuple-element.32, s32[64]{0:T(128)S(1)} %get-tuple-element.56, bf16[64,2,256]{2,1,0:T(2,128)(2,1)S(1)} %get-tuple-element.78), kind=kCustom, calls=%fused_computation.2 | custom fusion | bytes 196864 | tf_op jit(solution)/shard_map/scatter | solution.py:81
  54.0 1.5 fusion.84
  55.7 2.2 %fusion.90 = (f32[512]{0:T(512)S(1)}, f32[1536,512]{1,0:T(8,128)}) fusion(bf16[512,256]{1,0:T(8,128)(2,1)S(1)} %copy-done.5, bf16[1536,256]{1,0:T(8,128)(2,1)S(1)} %pad_maximum_fusion, pred[1536]{0:T(1024)(128)(4,1)S(1)} %get-tuple-element.63), kind=kOutput, calls=%fused_computation.139 | convolution fusion | flops 203685376 | bytes 3674112 | tf_op jit(solution)/shard_map/dot_general | solution.py:28
  58.5 7.5 %scatter_fusion.1 = bf16[512,2,256]{2,1,0:T(2,128)(2,1)} fusion(bf16[512,2,256]{2,1,0:T(2,128)(2,1)} %get-tuple-element.33, s32[64]{0:T(128)} %get-tuple-element.57, bf16[64,2,256]{2,1,0:T(2,128)(2,1)S(1)} %get-tuple-element.77), kind=kCustom, calls=%fused_computation.3 | custom fusion | bytes 196864 | tf_op jit(solution)/shard_map/scatter | solution.py:81
  66.0 2.1 %fusion.85 = (bf16[512,1,256]{2,1,0:T(2,128)(2,1)S(1)}, bf16[512,1,256]{2,1,0:T(2,128)(2,1)S(1)}) fusion(bf16[512,2,256]{2,1,0:T(2,128)(2,1)} %scatter_fusion.1), kind=kLoop, calls=%fused_computation.134 | loop fusion | bytes 1048576 | tf_op jit(solution)/shard_map/slice | solution.py:20
  68.2 1.1 pad_maximum_fusion.2
  70.9 1.0 copy-done.1
  76.9 0.7 pad_maximum_fusion.6
  77.8 103.7 %all-reduce.2.cloned.1.call-done = f32[2,512,64]{1,2,0:T(8,128)} async-done(((f32[2,512,64]{1,2,0:T(8,128)}), f32[2,512,64]{1,2,0:T(8,128)}) %all-reduce.2.cloned.1.call-update) | async-done | bytes 262160 | tf_op jit(solution)/shard_map/psum | solution.py:98
  181.5 0.9 fusion.72
  182.5 0.7 copy.67
  183.2 0.7 copy.66
  183.9 1.0 copy.88
  (81 shorter events, 11.4 us)
Async XLA Ops:
  7.2 7.2 %copy-start = (s32[64,2,64]{2,1,0:T(2,128)S(1)}, s32[64,2,64]{2,1,0:T(2,128)}, u32[]{:S(2)}) copy-start(s32[64,2,64]{2,1,0:T(2,128)} %param.19) | copy-start | bytes 98308
  7.2 11.0 %copy-start.20 = (s32[64]{0:T(128)S(1)}, s32[64]{0:T(128)}, u32[]{:S(2)}) copy-start(s32[64]{0:T(128)} %param.20) | copy-start | bytes 772
  7.2 11.1 %copy-start.19 = (s32[64,2]{0,1:T(2,128)S(1)}, s32[64,2]{0,1:T(2,128)}, u32[]{:S(2)}) copy-start(s32[64,2]{0,1:T(2,128)} %param.21) | copy-start | bytes 1540
  7.2 12.0 %copy-start.15 = (s32[64,2]{0,1:T(2,128)S(1)}, s32[64,2]{0,1:T(2,128)}, u32[]{:S(2)}) copy-start(s32[64,2]{0,1:T(2,128)} %param.18) | copy-start | bytes 1540
  7.2 15.2 %copy-start.13 = (bf16[1,2,512,256]{3,2,1,0:T(8,128)(2,1)S(1)}, bf16[1,2,512,256]{3,2,1,0:T(8,128)(2,1)}, u32[]{:S(2)}) copy-start(bf16[1,2,512,256]{3,2,1,0:T(8,128)(2,1)} %param.12) | copy-start | bytes 1572868
  7.2 174.3 %all-reduce.2.cloned.1.call-start = ((), (), s32[]{:S(2)}) async-start(), calls=%async_computation | async-start | bytes 524288 | tf_op jit(solution)/shard_map/psum | solution.py:98
  8.5 20.0 %collective-permute-start.1 = (bf16[1,2,256,2,256]{4,2,3,1,0:T(8,128)(2,1)S(1)}, bf16[1,2,256,2,256]{4,2,3,1,0:T(8,128)(2,1)}, u32[]{:S(2)}, u32[]{:S(2)}) collective-permute-start(bf16[1,2,256,2,256]{4,2,3,1,0:T(8,128)(2,1)S(1)} %copy.61), channel_id=1, source_target_pairs={{256,0},{264,8},{272,16},{280,24},{288,32},{296,40},{304,48},{312,... | collective-permute-start | bytes 1572872 | tf_op jit(solution)/shard_map/ppermute | solution.py:13
  12.0 34.5 %collective-permute-start = (bf16[1,2,512,2,256]{4,3,2,1,0:T(2,128)(2,1)}, bf16[1,2,512,2,256]{4,3,2,1,0:T(2,128)(2,1)S(1)}, u32[]{:S(2)}, u32[]{:S(2)}) collective-permute-start(bf16[1,2,512,2,256]{4,3,2,1,0:T(2,128)(2,1)} %param.13), channel_id=1, source_target_pairs={{256,0},{264,8},{272,16},{280,24},{288,32},{296,40},{304,48},{312,... | collective-permute-start | bytes 3145736 | tf_op jit(solution)/shard_map/ppermute | solution.py:13
  23.3 6.2 %copy-start.10 = (bf16[256,2,256]{2,0,1:T(8,128)(2,1)S(1)}, bf16[256,2,256]{2,0,1:T(8,128)(2,1)}, u32[]{:S(2)}) copy-start(bf16[256,2,256]{2,0,1:T(8,128)(2,1)} %get-tuple-element.44) | copy-start | bytes 786436
  23.4 6.2 %copy-start.11 = (bf16[256,2,256]{2,0,1:T(8,128)(2,1)S(1)}, bf16[256,2,256]{2,0,1:T(8,128)(2,1)}, u32[]{:S(2)}) copy-start(bf16[256,2,256]{2,0,1:T(8,128)(2,1)} %get-tuple-element.45) | copy-start | bytes 786436
  30.4 25.2 %copy-start.5 = (bf16[512,256]{1,0:T(8,128)(2,1)S(1)}, bf16[512,256]{1,0:T(8,128)(2,1)}, u32[]{:S(2)}) copy-start(bf16[512,256]{1,0:T(8,128)(2,1)} %get-tuple-element.40) | copy-start | bytes 786436
  46.5 9.2 %copy-start.2 = (bf16[1,2,512,2,256]{4,3,2,1,0:T(2,128)(2,1)}, bf16[1,2,512,2,256]{4,3,2,1,0:T(2,128)(2,1)S(1)}, u32[]{:S(2)}) copy-start(bf16[1,2,512,2,256]{4,3,2,1,0:T(2,128)(2,1)S(1)} %collective-permute-done) | copy-start | bytes 3145732
  55.5 2.3 %copy-start.6 = (bf16[512,256]{1,0:T(8,128)(2,1)S(1)}, bf16[512,256]{1,0:T(8,128)(2,1)}, u32[]{:S(2)}) copy-start(bf16[512,256]{1,0:T(8,128)(2,1)} %get-tuple-element.40) | copy-start | bytes 786436
  69.8 1.0 copy-start.4
  69.8 2.1 %copy-start.1 = (f32[1536,512]{1,0:T(8,128)S(1)}, f32[1536,512]{1,0:T(8,128)}, u32[]{:S(2)}) copy-start(f32[1536,512]{1,0:T(8,128)} %get-tuple-element.70) | copy-start | bytes 9437188
  70.5 1.9 %copy-start.8 = (bf16[512,256]{1,0:T(8,128)(2,1)S(1)}, bf16[512,256]{1,0:T(8,128)(2,1)}, u32[]{:S(2)}) copy-start(bf16[512,256]{1,0:T(8,128)(2,1)} %get-tuple-element.34) | copy-start | bytes 786436
  70.5 1.9 %copy-start.12 = (bf16[512,256]{1,0:T(8,128)(2,1)S(1)}, bf16[512,256]{1,0:T(8,128)(2,1)}, u32[]{:S(2)}) copy-start(bf16[512,256]{1,0:T(8,128)(2,1)} %get-tuple-element.76) | copy-start | bytes 786436
  73.6 1.1 copy-start.7
  73.6 1.1 copy-start.9
  75.4 1.2 copy-start.18
  75.9 1.8 copy-start.14
  75.9 1.9 copy-start.17
  75.9 105.6 %copy-start.16 = (f32[2]{0:T(128)S(1)}, f32[2]{0:T(128)}, u32[]{:S(2)}) copy-start(f32[2]{0:T(128)} %multiply_reduce_fusion) | copy-start | bytes 28
  75.9 108.0 %copy-start.3 = (bf16[1,2,512,2,256]{4,3,2,1,0:T(2,128)(2,1)S(1)}, bf16[1,2,512,2,256]{4,3,2,1,0:T(2,128)(2,1)}, u32[]{:S(2)}) copy-start(bf16[1,2,512,2,256]{4,3,2,1,0:T(2,128)(2,1)} %copy-done.2) | copy-start | bytes 3145732
Sparse Core Ops, SparseCore 0:
  77.8 103.7 all-reduce.1
where the time goes:
time: 192 us
  waiting for transfers between devices  120 us (62%)
  local copies, waits for them, and re-layouts  33.5 us (17%)
  between operations  14.5 us (8%)
  other arithmetic  11.1 us (6%)
  matrix products  6.91 us (4%)
  starting transfers between devices  5.88 us (3%)
    psum x1, waiting for transfers between devices, shards(): whole = lax.psum(partial_value, 'tp')  104 us
    ppermute x2, waiting for transfers between devices, from_behind(): return lax.ppermute(block, axis, route)  16.1 us
    scatter x2, local copies, waits for them, and re-layouts, shards(): stale_kv[0, slot_index].at[partner_lists[slot_index]]  10.2 us
    ppermute x2, starting transfers between devices, from_behind(): return lax.ppermute(block, axis, route)  5.85 us
    unnamed x51, local copies, waits for them, and re-layouts  5.25 us
    dot_general x4, matrix products, slot_velocity(): lax.dot_general(slot_query[:, first:first + HD], key_rows[:, first:first...  3.98 us
  transfers between devices with their start and end apart: 3, of which 2 were waited for; matrix products, arithmetic and copies ran while one was open for 8% of the time, Pallas kernels for 0%

commit v1 on v0

--- a/solution.py
+++ b/solution.py
@@ -1,3 +1,4 @@
+import functools
 import math
 import jax
 import jax.numpy as jnp
@@ -5,6 +6,13 @@
 from jax.sharding import PartitionSpec as P
 
 HD = 128
+
+
+def load_block(vals, axis_key):
+    return jnp.sum(lax.all_gather(vals, axis_key), 0)
+
+
+spots_render = functools.partial(load_block, axis_key="tp")
 
 
 def from_behind(block, axis, distance):
@@ -95,7 +103,7 @@
     tp_count = lax.axis_size("tp")
     share = partial_value.shape[1] // tp_count
     tp_index = lax.axis_index("tp")
-    whole = lax.psum(partial_value, "tp")
+    whole = spots_render(partial_value)
     summed = lax.dynamic_slice_in_dim(whole, tp_index * share, share, 1)
     row_ids = tp_index * share + jnp.arange(share, dtype=jnp.int32)
     live_rows = row_ids[None, :] < my_live[:, None]

time: 192 us -> 165 us (0.86)
  the two profiles are of different devices: /device:TPU:32 before, /device:TPU:2 now
where the time goes in v1:
time: 165 us; the launch traced here: 164 us
  waiting for transfers between devices  92 us (56%)
  local copies, waits for them, and re-layouts  32.4 us (20%)
  between operations  14.5 us (9%)
  other arithmetic  11.7 us (7%)
  matrix products  7.82 us (5%)
  starting transfers between devices  5.88 us (4%)
    all_gather x1, waiting for transfers between devices, load_block(): return jnp.sum(lax.all_gather(vals, axis_key), 0)  74 us
    ppermute x2, waiting for transfers between devices, from_behind(): return lax.ppermute(block, axis, route)  17.9 us
    scatter x2, local copies, waits for them, and re-layouts, shards(): stale_kv[0, slot_index].at[partner_lists[slot_index]]  10.2 us
    ppermute x2, starting transfers between devices, from_behind(): return lax.ppermute(block, axis, route)  5.85 us
    unnamed x47, local copies, waits for them, and re-layouts  5.18 us
    dot_general x4, matrix products, slot_velocity(): lax.dot_general(slot_query[:, first:first + HD], key_rows[:, first:first...  4.89 us
    slice x2, local copies, waits for them, and re-layouts, slot_velocity(): partner_kv[:, 1]  3.61 us
  transfers between devices with their start and end apart: 3, of which 2 were waited for; matrix products, arithmetic and copies ran while one was open for 9% of the time, Pallas kernels for 0%

profile of v1, /device:TPU:2, one launch (start us, length us, event | category | flops | bytes accessed | tf_op | source)
XLA Modules:
  0.0 164.3 jit_solution(16635053077995460322)
XLA Ops:
  7.2 1.1 copy.51
  8.4 3.5 %collective-permute-start.1 = (bf16[1,2,256,2,256]{4,2,3,1,0:T(8,128)(2,1)S(1)}, bf16[1,2,256,2,256]{4,2,3,1,0:T(8,128)(2,1)}, u32[]{:S(2)}, u32[]{:S(2)}) collective-permute-start(bf16[1,2,256,2,256]{4,2,3,1,0:T(8,128)(2,1)S(1)} %copy.51), channel_id=1, source_target_pairs={{256,0},{264,8},{272,16},{280,24},{288,32},{296,40},{304,48},{312,... | collective-permute-start | bytes 1572872 | tf_op jit(solution)/shard_map/ppermute | solution.py:21
  11.8 2.4 %collective-permute-start = (bf16[1,2,512,2,256]{4,3,2,1,0:T(2,128)(2,1)}, bf16[1,2,512,2,256]{4,3,2,1,0:T(2,128)(2,1)S(1)}, u32[]{:S(2)}, u32[]{:S(2)}) collective-permute-start(bf16[1,2,512,2,256]{4,3,2,1,0:T(2,128)(2,1)} %param.13), channel_id=1, source_target_pairs={{256,0},{264,8},{272,16},{280,24},{288,32},{296,40},{304,48},{312,... | collective-permute-start | bytes 3145736 | tf_op jit(solution)/shard_map/ppermute | solution.py:21
  15.3 0.7 slice_bitcast_fusion.10
  16.0 1.9 %fusion.83 = (bf16[1,1,512,2,256]{4,3,2,1,0:T(2,128)(2,1)S(1)}, bf16[1,1,512,2,256]{4,3,2,1,0:T(2,128)(2,1)S(1)}) fusion(bf16[1,2,512,2,256]{4,3,2,1,0:T(2,128)(2,1)} %param.13), kind=kLoop, calls=%fused_computation.132 | loop fusion | bytes 2097152 | tf_op jit(solution)/shard_map/slice | solution.py:94
  18.0 0.8 fusion.82
  20.6 0.7 iota_compare_fusion
  21.3 1.1 slice_bitcast_fusion.13
  22.6 0.8 slice_bitcast_fusion.4
  24.1 0.7 slice_bitcast_fusion.8
  24.8 1.5 slice_bitcast_fusion.3
  26.4 1.1 slice_bitcast_fusion.9
  27.4 1.0 fusion.60
  28.4 17.9 %collective-permute-done = bf16[1,2,512,2,256]{4,3,2,1,0:T(2,128)(2,1)S(1)} collective-permute-done((bf16[1,2,512,2,256]{4,3,2,1,0:T(2,128)(2,1)}, bf16[1,2,512,2,256]{4,3,2,1,0:T(2,128)(2,1)S(1)}, u32[]{:S(2)}, u32[]{:S(2)}) %collective-permute-start) | collective-permute-done | bytes 1048608 | tf_op jit(solution)/shard_map/ppermute | solution.py:21
  46.4 1.5 slice_bitcast_fusion.1
  47.9 1.8 %gather_fusion = bf16[64,2,256]{2,1,0:T(2,128)(2,1)S(1)} fusion(bf16[512,2,256]{2,1,0:T(2,128)(2,1)} %get-tuple-element.15, s32[1024]{0:T(1024)S(1)} %pad_clamp_fusion.1), kind=kCustom, calls=%fused_computation.clone | custom fusion | bytes 131328 | tf_op jit(solution)/shard_map/jit(_take)/gather | solution.py:83
  49.7 0.7 gather_fusion.1
  50.4 0.9 broadcast_select_fusion
  51.3 2.6 %scatter_fusion = bf16[512,2,256]{2,1,0:T(2,128)(2,1)S(1)} fusion(bf16[512,2,256]{2,1,0:T(2,128)(2,1)S(1)} %get-tuple-element.17, s32[64]{0:T(128)S(1)} %get-tuple-element.41, bf16[64,2,256]{2,1,0:T(2,128)(2,1)S(1)} %get-tuple-element.63), kind=kCustom, calls=%fused_computation.2 | custom fusion | bytes 196864 | tf_op jit(solution)/shard_map/scatter | solution.py:89
  53.9 1.5 fusion.84
  55.6 2.2 %fusion.90 = (f32[512]{0:T(512)S(1)}, f32[1536,512]{1,0:T(8,128)}) fusion(bf16[512,256]{1,0:T(8,128)(2,1)S(1)} %get-tuple-element.25, bf16[1536,256]{1,0:T(8,128)(2,1)S(1)} %pad_maximum_fusion, pred[1536]{0:T(1024)(128)(4,1)S(1)} %get-tuple-element.48), kind=kOutput, calls=%fused_computation.139 | convolution fusion | flops 203685376 | bytes 3674112 | tf_op jit(solution)/shard_map/dot_general | solution.py:36
  57.8 1.5 fusion.91
  59.3 7.5 %scatter_fusion.1 = bf16[512,2,256]{2,1,0:T(2,128)(2,1)} fusion(bf16[512,2,256]{2,1,0:T(2,128)(2,1)} %get-tuple-element.18, s32[64]{0:T(128)} %get-tuple-element.42, bf16[64,2,256]{2,1,0:T(2,128)(2,1)S(1)} %get-tuple-element.62), kind=kCustom, calls=%fused_computation.3 | custom fusion | bytes 196864 | tf_op jit(solution)/shard_map/scatter | solution.py:89
  66.8 2.1 %fusion.85 = (bf16[512,1,256]{2,1,0:T(2,128)(2,1)S(1)}, bf16[512,1,256]{2,1,0:T(2,128)(2,1)S(1)}) fusion(bf16[512,2,256]{2,1,0:T(2,128)(2,1)} %scatter_fusion.1), kind=kLoop, calls=%fused_computation.134 | loop fusion | bytes 1048576 | tf_op jit(solution)/shard_map/slice | solution.py:28
  68.9 1.1 pad_maximum_fusion.2
  71.7 1.0 copy-done.1
  77.7 0.7 pad_maximum_fusion.6
  79.1 74.0 %all-gather.3.cloned.1.call-done = f32[16,512,64]{1,2,0:T(8,128)} async-done(((f32[2,512,64]{1,2,0:T(8,128)}), f32[16,512,64]{1,2,0:T(8,128)}) %all-gather.3.cloned.1.call-update) | async-done | bytes 2097168 | tf_op jit(solution)/shard_map/all_gather | solution.py:12
  153.1 1.8 %reduce_sum.49 = f32[2,512,64]{1,2,0:T(8,128)S(1)} reduce(f32[8,2,512,64]{2,3,1,0:T(8,128)} %bitcast.88, f32[]{:T(128)} %constant.66.clone.1), dimensions={0}, to_apply=%region_10.12 | reduce | flops 458752 | bytes 2359300 | tf_op jit(solution)/shard_map/reduce_sum | solution.py:12
  155.0 0.7 copy.57
  155.7 0.7 copy.56
  156.5 1.0 copy.77
  (78 shorter events, 11.2 us)
Async XLA Ops:
  7.2 7.1 %copy-start = (s32[64,2,64]{2,1,0:T(2,128)S(1)}, s32[64,2,64]{2,1,0:T(2,128)}, u32[]{:S(2)}) copy-start(s32[64,2,64]{2,1,0:T(2,128)} %param.19) | copy-start | bytes 98308
  7.2 10.8 %copy-start.14 = (s32[64,2]{0,1:T(2,128)S(1)}, s32[64,2]{0,1:T(2,128)}, u32[]{:S(2)}) copy-start(s32[64,2]{0,1:T(2,128)} %param.18) | copy-start | bytes 1540
  7.2 145.9 %all-gather.3.cloned.1.call-start = ((), (), s32[]{:S(2)}) async-start(), calls=%async_computation | async-start | bytes 2359296 | tf_op jit(solution)/shard_map/all_gather | solution.py:12
  8.4 18.0 %collective-permute-start.1 = (bf16[1,2,256,2,256]{4,2,3,1,0:T(8,128)(2,1)S(1)}, bf16[1,2,256,2,256]{4,2,3,1,0:T(8,128)(2,1)}, u32[]{:S(2)}, u32[]{:S(2)}) collective-permute-start(bf16[1,2,256,2,256]{4,2,3,1,0:T(8,128)(2,1)S(1)} %copy.51), channel_id=1, source_target_pairs={{256,0},{264,8},{272,16},{280,24},{288,32},{296,40},{304,48},{312,... | collective-permute-start | bytes 1572872 | tf_op jit(solution)/shard_map/ppermute | solution.py:21
  11.8 34.5 %collective-permute-start = (bf16[1,2,512,2,256]{4,3,2,1,0:T(2,128)(2,1)}, bf16[1,2,512,2,256]{4,3,2,1,0:T(2,128)(2,1)S(1)}, u32[]{:S(2)}, u32[]{:S(2)}) collective-permute-start(bf16[1,2,512,2,256]{4,3,2,1,0:T(2,128)(2,1)} %param.13), channel_id=1, source_target_pairs={{256,0},{264,8},{272,16},{280,24},{288,32},{296,40},{304,48},{312,... | collective-permute-start | bytes 3145736 | tf_op jit(solution)/shard_map/ppermute | solution.py:21
  18.0 6.9 %copy-start.5 = (bf16[1,2,512,2,256]{4,3,2,1,0:T(2,128)(2,1)S(1)}, bf16[1,2,512,2,256]{4,3,2,1,0:T(2,128)(2,1)}, u32[]{:S(2)}) copy-start(bf16[1,2,512,2,256]{4,3,2,1,0:T(2,128)(2,1)} %param.14) | copy-start | bytes 3145732
  22.4 33.1 %copy-start.6 = (bf16[512,256]{1,0:T(8,128)(2,1)}, bf16[512,256]{1,0:T(8,128)(2,1)S(1)}, u32[]{:S(2)}) copy-start(bf16[512,256]{1,0:T(8,128)(2,1)S(1)} %get-tuple-element.25) | copy-start | bytes 786436
  22.6 4.9 %copy-start.11 = (bf16[256,2,256]{2,0,1:T(8,128)(2,1)S(1)}, bf16[256,2,256]{2,0,1:T(8,128)(2,1)}, u32[]{:S(2)}) copy-start(bf16[256,2,256]{2,0,1:T(8,128)(2,1)} %get-tuple-element.30) | copy-start | bytes 786436
  28.4 27.0 %copy-start.12 = (bf16[512,256]{1,0:T(8,128)(2,1)S(1)}, bf16[512,256]{1,0:T(8,128)(2,1)}, u32[]{:S(2)}) copy-start(bf16[512,256]{1,0:T(8,128)(2,1)} %get-tuple-element.60) | copy-start | bytes 786436
  46.4 9.2 %copy-start.2 = (bf16[1,2,512,2,256]{4,3,2,1,0:T(2,128)(2,1)}, bf16[1,2,512,2,256]{4,3,2,1,0:T(2,128)(2,1)S(1)}, u32[]{:S(2)}) copy-start(bf16[1,2,512,2,256]{4,3,2,1,0:T(2,128)(2,1)S(1)} %collective-permute-done) | copy-start | bytes 3145732
  70.6 1.0 copy-start.4
  70.6 2.1 %copy-start.1 = (f32[1536,512]{1,0:T(8,128)S(1)}, f32[1536,512]{1,0:T(8,128)}, u32[]{:S(2)}) copy-start(f32[1536,512]{1,0:T(8,128)} %get-tuple-element.55) | copy-start | bytes 9437188
  71.2 1.9 %copy-start.8 = (bf16[512,256]{1,0:T(8,128)(2,1)S(1)}, bf16[512,256]{1,0:T(8,128)(2,1)}, u32[]{:S(2)}) copy-start(bf16[512,256]{1,0:T(8,128)(2,1)} %get-tuple-element.19) | copy-start | bytes 786436
  71.2 1.9 %copy-start.10 = (bf16[512,256]{1,0:T(8,128)(2,1)S(1)}, bf16[512,256]{1,0:T(8,128)(2,1)}, u32[]{:S(2)}) copy-start(bf16[512,256]{1,0:T(8,128)(2,1)} %get-tuple-element.61) | copy-start | bytes 786436
  74.4 1.1 copy-start.7
  74.4 1.1 copy-start.9
  76.2 1.2 copy-start.16
  76.7 1.8 %copy-start.13 = (f32[1,2,64,64]{3,2,1,0:T(8,128)S(1)}, f32[1,2,64,64]{3,2,1,0:T(8,128)}, u32[]{:S(2)}) copy-start(f32[1,2,64,64]{3,2,1,0:T(8,128)} %param.17) | copy-start | bytes 98308
  76.7 1.9 %copy-start.18 = (s32[64]{0:T(128)S(1)}, s32[64]{0:T(128)}, u32[]{:S(2)}) copy-start(s32[64]{0:T(128)} %param.20) | copy-start | bytes 772
  76.7 1.9 %copy-start.17 = (s32[64,2]{0,1:T(2,128)S(1)}, s32[64,2]{0,1:T(2,128)}, u32[]{:S(2)}) copy-start(s32[64,2]{0,1:T(2,128)} %param.21) | copy-start | bytes 1540
  76.7 2.3 %copy-start.15 = (s32[2]{0:T(128)S(1)}, s32[2]{0:T(128)}, u32[]{:S(2)}) copy-start(s32[2]{0:T(128)} %get-tuple-element.7) | copy-start | bytes 28
  77.3 79.1 %copy-start.3 = (bf16[1,2,512,2,256]{4,3,2,1,0:T(2,128)(2,1)S(1)}, bf16[1,2,512,2,256]{4,3,2,1,0:T(2,128)(2,1)}, u32[]{:S(2)}) copy-start(bf16[1,2,512,2,256]{4,3,2,1,0:T(2,128)(2,1)} %copy-done.2) | copy-start | bytes 3145732
Sparse Core Ops, SparseCore 0:
  78.6 74.5 all-gather.2
